TPU v7x, 32 devices: a whole 2x2x4 slice. The times are simulated.
32 devices in a mesh: nodes: 8 (over z, y), mp: 4 (over x, core).
Axes of the slice: x: 2, y: 2, z: 4, core: 2. Of those that a mesh axis runs over, the one named last changes fastest.
Arguments:
- query: bfloat16 [2048, 512], P('nodes', 'mp'), may hold values from -240 to 240
- key: bfloat16 [2048, 512], P('nodes', 'mp'), may hold values from -7 to 7
- value: bfloat16 [2048, 512], P('nodes', 'mp'), may hold values from -12 to 12
- out_weight: bfloat16 [512, 512], P('mp'), may hold values from -0.25 to 0.25
- cotangent: bfloat16 [2048, 512], P('nodes', 'mp'), may hold values from -6 to 6
- virtual_key: bfloat16 [64, 512], P('nodes', 'mp'), may hold values from -6 to 6
- virtual_value: bfloat16 [64, 512], P('nodes', 'mp'), may hold values from -12 to 12
- halo_rows: int32 [8, 2, 128], P('nodes'), may hold values from 0 to 255
- halo_live: int32 [8, 2], P('nodes'), may hold values from 64 to 128, as said below
- expand_rows: int32 [8, 8, 2], P('nodes'), may hold values from 0 to 255
- local_mask: int32 [16, 4], P('nodes'), may hold values from 0 to 1, as said below
- expand_mask: int32 [16, 8], P('nodes'), may hold values 0 or 1
Outputs:
- output: bfloat16 [2048, 512], P('nodes', 'mp')
- grad_query: float32 [2048, 512], P('nodes', 'mp')
- grad_key: float32 [2048, 512], P('nodes', 'mp')
- grad_value: float32 [2048, 512], P('nodes', 'mp')
- grad_virtual_key: float32 [64, 512], P('nodes', 'mp')
- grad_virtual_value: float32 [64, 512], P('nodes', 'mp')
Inputs may be any that keep to these rules, and one draw needn't show every extreme that they name: halo_rows[p, 0, :] index nodes of partition p (0 to 255) sent to partition p + 1, halo_rows[p, 1, :] those sent to partition p - 1; repeats possible. Only the leading halo_live slots of what a partition receives from a neighbour are edges; the value 128 occurs in every draw. expand_rows[r, p, :] index nodes of partition r. Every query tile attends its own tile and both received boundary tiles: local_mask[t, t mod 2], local_mask[t, 2] and local_mask[t, 3] are 1.
All inputs are finite; a program needn't handle non-finite values. No bound on the sum of `expand_mask` on one device may be relied on, other than what follows from the above.
Results may differ from a plain program's by a relative error of at most 0.034.
Values may be sent and summed in bfloat16 or wider, within the bound.
A program may use at most 64 MiB of HBM per device.

v0:
```python
import jax
import jax.numpy as jnp
from jax import lax
from jax.sharding import PartitionSpec as P

HEADS = 8


def extended(array, sides, width):
    for axis, dim in sides:
        devices, length = (lax.axis_size(axis), array.shape[dim])
        up = [(i, (i + 1) % devices) for i in range(devices)]
        down = [(j, i) for i, j in up]
        last = lax.slice_in_dim(array, length - width, length, axis=dim)
        leading = lax.slice_in_dim(array, 0, width, axis=dim)
        before = lax.ppermute(last, axis, up)
        after = lax.ppermute(leading, axis, down)
        array = jnp.concatenate([before, array, after], axis=dim)
    return array


def edge_mask(local_block, expand_block, live, tile_rows, halo_cap, exp_slot, virtual_count):
    tile_count = local_block.shape[0]
    own_tiles = jnp.repeat(
        jnp.repeat(local_block[:, :tile_count] > 0, tile_rows, axis=0), tile_rows, axis=1
    )
    slot_index = jnp.arange(halo_cap)
    left_ok = (local_block[:, tile_count] > 0)[:, None] & (slot_index < live[0])[None, :]
    right_ok = (local_block[:, tile_count + 1] > 0)[:, None] & (slot_index < live[1])[None, :]
    expand_ok = jnp.repeat(expand_block > 0, exp_slot, axis=1)
    remote_tiles = jnp.repeat(
        jnp.concatenate([left_ok, right_ok, expand_ok], axis=1), tile_rows, axis=0
    )
    virtual_ok = jnp.ones((tile_count * tile_rows, virtual_count), dtype=jnp.bool_)
    return jnp.concatenate([own_tiles, remote_tiles, virtual_ok], axis=1)


def body(
    query,
    key,
    value,
    out_weight,
    cotangent,
    virtual_key,
    virtual_value,
    halo_rows,
    halo_live,
    expand_rows,
    local_mask,
    expand_mask,
):
    node_rows, width = query.shape
    heads_dev = HEADS // lax.axis_size("mp")
    head_dim = width // heads_dev
    score_scale = head_dim ** (-0.5)
    tile_count = local_mask.shape[0]
    tile_rows = node_rows // tile_count
    halo_cap = halo_rows.shape[2]
    peer_count = expand_rows.shape[1]
    exp_slot = expand_rows.shape[2]
    to_right = halo_rows[0, 0]
    to_left = halo_rows[0, 1]
    expand_flat = expand_rows[0].reshape(-1)
    key_value = jnp.concatenate([key, value], axis=1)
    outgoing_rows = jnp.concatenate([key_value[to_left], key_value[to_right]], axis=0)
    padded = extended(outgoing_rows, (("nodes", 0),), halo_cap)
    from_left = padded[:halo_cap]
    from_right = padded[3 * halo_cap :]
    expand_sent = key_value[expand_flat].reshape(peer_count, exp_slot, 2 * width)
    arrived = lax.all_to_all(expand_sent, "nodes", split_axis=0, concat_axis=0, tiled=True).reshape(
        peer_count * exp_slot, 2 * width
    )
    all_virtual_key, all_virtual_value = (
        lax.all_gather(virtual_key, "nodes", axis=0, tiled=True),
        lax.all_gather(virtual_value, "nodes", axis=0, tiled=True),
    )
    virtual_count = all_virtual_key.shape[0]
    all_keys = jnp.concatenate(
        [key, from_left[:, :width], from_right[:, :width], arrived[:, :width], all_virtual_key],
        axis=0,
    )
    all_values = jnp.concatenate(
        [value, from_left[:, width:], from_right[:, width:], arrived[:, width:], all_virtual_value],
        axis=0,
    )
    allowed = edge_mask(
        local_mask, expand_mask, halo_live[0], tile_rows, halo_cap, exp_slot, virtual_count
    )
    d_attn = jnp.einsum(
        "nc,wc->nw",
        lax.all_gather(cotangent, "mp", axis=1, tiled=True),
        out_weight,
        preferred_element_type=jnp.float32,
    ).astype(jnp.bfloat16)
    attn_parts = []
    grad_query_parts = []
    grad_key_parts = []
    grad_value_parts = []
    for head_number in range(heads_dev):
        low = head_number * head_dim
        high = low + head_dim
        query_head = query[:, low:high]
        key_head = all_keys[:, low:high]
        value_head = all_values[:, low:high]
        grad_head = d_attn[:, low:high]
        scores = (
            jnp.einsum("qd,kd->qk", query_head, key_head, preferred_element_type=jnp.float32)
            * score_scale
        )
        scores = jnp.where(allowed, scores, -1e30)
        row_max = jnp.max(scores, axis=1, keepdims=True)
        weights = jnp.exp(scores - row_max)
        probs = weights / jnp.sum(weights, axis=1, keepdims=True)
        probs_b = probs.astype(jnp.bfloat16)
        attn_head = jnp.dot(probs_b, value_head, preferred_element_type=jnp.float32).astype(
            jnp.bfloat16
        )
        d_prob = jnp.einsum("qd,kd->qk", grad_head, value_head, preferred_element_type=jnp.float32)
        row_delta = jnp.sum(
            grad_head.astype(jnp.float32) * attn_head.astype(jnp.float32), axis=1, keepdims=True
        )
        d_score = (probs * (d_prob - row_delta) * score_scale).astype(jnp.bfloat16)
        attn_parts.append(attn_head)
        grad_query_parts.append(jnp.dot(d_score, key_head, preferred_element_type=jnp.float32))
        grad_key_parts.append(
            jnp.einsum("qk,qd->kd", d_score, query_head, preferred_element_type=jnp.float32)
        )
        grad_value_parts.append(
            jnp.einsum("qk,qd->kd", probs_b, grad_head, preferred_element_type=jnp.float32)
        )
    attn = jnp.concatenate(attn_parts, axis=1)
    grad_query = jnp.concatenate(grad_query_parts, axis=1)
    grad_keys = jnp.concatenate(grad_key_parts, axis=1)
    grad_values = jnp.concatenate(grad_value_parts, axis=1)
    projected = jnp.dot(attn, out_weight, preferred_element_type=jnp.float32)
    output = lax.psum_scatter(projected, "mp", scatter_dimension=1, tiled=True).astype(jnp.bfloat16)
    left_end = node_rows + halo_cap
    right_end = left_end + halo_cap
    expand_end = right_end + peer_count * exp_slot
    grad_pairs = jnp.concatenate([grad_keys, grad_values], axis=1)
    halo_back = grad_pairs[node_rows:right_end]
    returned = extended(halo_back, (("nodes", 0),), halo_cap)
    for_left_sent = returned[:halo_cap]
    for_right_sent = returned[3 * halo_cap :]
    expand_back = grad_pairs[right_end:expand_end].reshape(peer_count, exp_slot, 2 * width)
    came_home = lax.all_to_all(
        expand_back, "nodes", split_axis=0, concat_axis=0, tiled=True
    ).reshape(peer_count * exp_slot, 2 * width)
    own_grads = grad_pairs[:node_rows]
    own_grads = own_grads.at[to_left].add(for_left_sent)
    own_grads = own_grads.at[to_right].add(for_right_sent)
    own_grads = own_grads.at[expand_flat].add(came_home)
    grad_key = own_grads[:, :width]
    grad_value = own_grads[:, width:]
    virtual_key_term = grad_keys[expand_end:]
    virtual_value_term = grad_values[expand_end:]
    grad_virtual_key, grad_virtual_value = (
        lax.psum_scatter(virtual_key_term, "nodes", scatter_dimension=0, tiled=True),
        lax.psum_scatter(virtual_value_term, "nodes", scatter_dimension=0, tiled=True),
    )
    return (output, grad_query, grad_key, grad_value, grad_virtual_key, grad_virtual_value)


def solution(mesh):
    return jax.shard_map(
        body,
        mesh=mesh,
        in_specs=(
            P("nodes", "mp"),
            P("nodes", "mp"),
            P("nodes", "mp"),
            P("mp", None),
            P("nodes", "mp"),
            P("nodes", "mp"),
            P("nodes", "mp"),
            P("nodes", None, None),
            P("nodes", None),
            P("nodes", None, None),
            P("nodes", None),
            P("nodes", None),
        ),
        out_specs=(
            P("nodes", "mp"),
            P("nodes", "mp"),
            P("nodes", "mp"),
            P("nodes", "mp"),
            P("nodes", "mp"),
            P("nodes", "mp"),
        ),
        check_vma=False,
    )
```

profile of v0, /device:TPU:0, one launch (start us, length us, event | category | flops | bytes accessed | tf_op | source)
XLA Modules:
  0.0 192.0 jit_solution(5253378758399897791)
XLA Ops:
  8.0 0.8 copy.38
  8.9 0.9 constant_dynamic-update-slice_fusion.1
  11.0 7.4 %all-to-all-start = ((bf16[8,2,256]{2,1,0:T(2,128)(2,1)}), bf16[8,2,256]{2,1,0:T(2,128)(2,1)S(1)}, u32[]{:S(2)}, u32[]{:S(2)}) async-start(bf16[8,2,256]{2,1,0:T(2,128)(2,1)} %reshape.142), calls=%async_computation | async-start | bytes 16384 | tf_op jit(solution)/shard_map/all_to_all | solution.py:70
  18.5 0.8 gather_fusion
  19.3 2.1 %collective-permute-start = (bf16[128,256]{1,0:T(8,128)(2,1)S(1)}, bf16[128,256]{1,0:T(8,128)(2,1)S(1)}, u32[]{:S(2)}, u32[]{:S(2)}) collective-permute-start(bf16[128,256]{1,0:T(8,128)(2,1)S(1)} %gather_fusion), channel_id=1, source_target_pairs={{0,4},{4,8},{8,12},{12,16},{16,20},{20,24},{24,28},{28,0},{1,5},{5... | collective-permute-start | bytes 196616 | tf_op jit(solution)/shard_map/ppermute | solution.py:16
  21.4 0.8 gather_fusion.1
  22.3 2.8 %collective-permute-start.1 = (bf16[128,256]{1,0:T(8,128)(2,1)S(1)}, bf16[128,256]{1,0:T(8,128)(2,1)S(1)}, u32[]{:S(2)}, u32[]{:S(2)}) collective-permute-start(bf16[128,256]{1,0:T(8,128)(2,1)S(1)} %gather_fusion.1), channel_id=1, source_target_pairs={{4,0},{8,4},{12,8},{16,12},{20,16},{24,20},{28,24},{0,28},{5,1},{9... | collective-permute-start | bytes 196616 | tf_op jit(solution)/shard_map/ppermute | solution.py:17
  28.6 5.8 %all_gather.11 = bf16[256,512]{1,0:T(8,128)(2,1)S(1)} all-gather(bf16[256,128]{1,0:T(8,128)(2,1)S(1)} %copy-done.3), channel_id=1, replica_groups=mesh['nodes'=8,'mp'=4] {'mp'}, dimensions={1}, use_global_device_ids=true | all-gather | bytes 327680 | tf_op jit(solution)/shard_map/all_gather | solution.py:91
  37.5 26.1 %all_gather.9 = bf16[64,128]{1,0:T(8,128)(2,1)S(1)} all-gather(bf16[8,128]{1,0:T(8,128)(2,1)S(1)} %copy-done.6), channel_id=1, replica_groups=mesh['nodes'=8,'mp'=4] {'nodes'}, dimensions={0}, use_global_device_ids=true | all-gather | bytes 18432 | tf_op jit(solution)/shard_map/all_gather | solution.py:74
  63.7 26.0 %all_gather.10 = bf16[64,128]{1,0:T(8,128)(2,1)S(1)} all-gather(bf16[8,128]{1,0:T(8,128)(2,1)S(1)} %copy-done.7), channel_id=1, replica_groups=mesh['nodes'=8,'mp'=4] {'nodes'}, dimensions={0}, use_global_device_ids=true | all-gather | bytes 18432 | tf_op jit(solution)/shard_map/all_gather | solution.py:75
  89.8 0.8 copy-done.1
  93.8 0.7 pad_maximum_fusion.6
  94.6 0.7 pad_maximum_fusion.5
  96.0 3.3 %all-to-all-start.1 = ((f32[8,2,256]{2,1,0:T(2,128)}), f32[8,2,256]{2,1,0:T(2,128)S(1)}, u32[]{:S(2)}, u32[]{:S(2)}) async-start(f32[8,2,256]{2,1,0:T(2,128)} %reshape.144), calls=%async_computation.2 | async-start | bytes 32768 | tf_op jit(solution)/shard_map/all_to_all | solution.py:146
  99.4 1.0 fusion.26
  101.7 0.8 copy.43
  102.6 4.7 %collective-permute-start.3 = (f32[128,256]{0,1:T(8,128)S(1)}, f32[128,256]{0,1:T(8,128)S(1)}, u32[]{:S(2)}, u32[]{:S(2)}) collective-permute-start(f32[128,256]{0,1:T(8,128)S(1)} %get-tuple-element.30), channel_id=1, source_target_pairs={{4,0},{8,4},{12,8},{16,12},{20,16},{24,20},{28,24},{0,28},{5,1},{9... | collective-permute-start | bytes 393224 | tf_op jit(solution)/shard_map/ppermute | solution.py:17
  107.3 68.6 %all-reduce.5.cloned.1.call-done = (f32[64,128]{0,1:T(8,128)}, f32[64,128]{0,1:T(8,128)}) async-done(((f32[64,128]{0,1:T(8,128)}, f32[64,128]{0,1:T(8,128)}), (f32[64,128]{0,1:T(8,128)}, f32[64,128]{0,1:T(8,128)})) %all-reduce.5.cloned.1.call-update) | async-done | bytes 65552
  175.9 0.9 constant_dynamic-slice_fusion.1
  178.5 1.4 scatter_fusion
  180.1 1.4 scatter_fusion.1
  181.5 0.8 scatter_fusion.2
  182.3 0.7 fusion.46
  183.0 1.5 convert_element_type.40
  (100 shorter events, 14.5 us)
Async XLA Ops:
  8.0 26.4 %copy-start = (bf16[128,512]{1,0:T(8,128)(2,1)S(1)}, bf16[128,512]{1,0:T(8,128)(2,1)}, u32[]{:S(2)}) copy-start(bf16[128,512]{1,0:T(8,128)(2,1)} %param.15) | copy-start | bytes 393220
  8.9 0.9 copy-start.2
  11.0 7.4 %copy-start.9 = (s32[1,2,128]{2,1,0:T(2,128)S(1)}, s32[1,2,128]{2,1,0:T(2,128)}, u32[]{:S(2)}) copy-start(s32[1,2,128]{2,1,0:T(2,128)} %param.19) | copy-start | bytes 3076
  11.0 78.6 %all-to-all-start = ((bf16[8,2,256]{2,1,0:T(2,128)(2,1)}), bf16[8,2,256]{2,1,0:T(2,128)(2,1)S(1)}, u32[]{:S(2)}, u32[]{:S(2)}) async-start(bf16[8,2,256]{2,1,0:T(2,128)(2,1)} %reshape.142), calls=%async_computation | async-start | bytes 16384 | tf_op jit(solution)/shard_map/all_to_all | solution.py:70
  19.3 70.3 %collective-permute-start = (bf16[128,256]{1,0:T(8,128)(2,1)S(1)}, bf16[128,256]{1,0:T(8,128)(2,1)S(1)}, u32[]{:S(2)}, u32[]{:S(2)}) collective-permute-start(bf16[128,256]{1,0:T(8,128)(2,1)S(1)} %gather_fusion), channel_id=1, source_target_pairs={{0,4},{4,8},{8,12},{12,16},{16,20},{20,24},{24,28},{28,0},{1,5},{5... | collective-permute-start | bytes 196616 | tf_op jit(solution)/shard_map/ppermute | solution.py:16
  21.4 3.6 %copy-start.5 = (s32[2,4]{1,0:T(2,128)S(1)}, s32[2,4]{1,0:T(2,128)}, u32[]{:S(2)}) copy-start(s32[2,4]{1,0:T(2,128)} %param.22) | copy-start | bytes 100
  21.4 7.2 %copy-start.3 = (bf16[256,128]{1,0:T(8,128)(2,1)S(1)}, bf16[256,128]{1,0:T(8,128)(2,1)}, u32[]{:S(2)}) copy-start(bf16[256,128]{1,0:T(8,128)(2,1)} %param.16) | copy-start | bytes 196612
  22.3 67.4 %collective-permute-start.1 = (bf16[128,256]{1,0:T(8,128)(2,1)S(1)}, bf16[128,256]{1,0:T(8,128)(2,1)S(1)}, u32[]{:S(2)}, u32[]{:S(2)}) collective-permute-start(bf16[128,256]{1,0:T(8,128)(2,1)S(1)} %gather_fusion.1), channel_id=1, source_target_pairs={{4,0},{8,4},{12,8},{16,12},{20,16},{24,20},{28,24},{0,28},{5,1},{9... | collective-permute-start | bytes 196616 | tf_op jit(solution)/shard_map/ppermute | solution.py:17
  25.1 0.7 copy-start.10
  25.9 0.7 copy-start.8
  35.0 0.7 copy-start.11
  36.9 0.7 copy-start.6
  37.5 26.1 %copy-start.7 = (bf16[8,128]{1,0:T(8,128)(2,1)S(1)}, bf16[8,128]{1,0:T(8,128)(2,1)}, u32[]{:S(2)}) copy-start(bf16[8,128]{1,0:T(8,128)(2,1)} %param.18) | copy-start | bytes 6148
  89.7 0.8 copy-start.1
  96.0 11.2 %all-to-all-start.1 = ((f32[8,2,256]{2,1,0:T(2,128)}), f32[8,2,256]{2,1,0:T(2,128)S(1)}, u32[]{:S(2)}, u32[]{:S(2)}) async-start(f32[8,2,256]{2,1,0:T(2,128)} %reshape.144), calls=%async_computation.2 | async-start | bytes 32768 | tf_op jit(solution)/shard_map/all_to_all | solution.py:146
  99.4 76.5 %all-reduce.5.cloned.1.call-start = ((), (), s32[]{:S(2)}) async-start(), calls=%async_computation.4 | async-start | bytes 262144
  100.5 82.5 %reduce-scatter.4.cloned.1.call-start = ((), (), s32[]{:S(2)}) async-start(), calls=%async_computation.3 | async-start | bytes 655360 | tf_op jit(solution)/shard_map/reduce_scatter | solution.py:136
  102.6 77.4 %collective-permute-start.3 = (f32[128,256]{0,1:T(8,128)S(1)}, f32[128,256]{0,1:T(8,128)S(1)}, u32[]{:S(2)}, u32[]{:S(2)}) collective-permute-start(f32[128,256]{0,1:T(8,128)S(1)} %get-tuple-element.30), channel_id=1, source_target_pairs={{4,0},{8,4},{12,8},{16,12},{20,16},{24,20},{28,24},{0,28},{5,1},{9... | collective-permute-start | bytes 393224 | tf_op jit(solution)/shard_map/ppermute | solution.py:17
  107.2 71.2 %collective-permute-start.2 = (f32[128,256]{0,1:T(8,128)S(1)}, f32[128,256]{0,1:T(8,128)S(1)}, u32[]{:S(2)}, u32[]{:S(2)}) collective-permute-start(f32[128,256]{0,1:T(8,128)S(1)} %get-tuple-element.31), channel_id=1, source_target_pairs={{0,4},{4,8},{8,12},{12,16},{16,20},{20,24},{24,28},{28,0},{1,5},{5... | collective-permute-start | bytes 393224 | tf_op jit(solution)/shard_map/ppermute | solution.py:16
  176.8 0.8 copy-start.4
Sparse Core Ops, SparseCore 0:
  104.7 71.2 all-reduce.4
Sparse Core Ops, SparseCore 1:
  103.5 22.9 reduce-scatter.3
where the time goes:
time: 193 us; the launch traced here: 192 us
  waiting for transfers between devices  69.2 us (36%)
  blocking collectives  57.9 us (30%)
  starting transfers between devices  20.4 us (11%)
  between operations  16.5 us (9%)
  local copies, waits for them, and re-layouts  14.7 us (8%)
  other arithmetic  8.82 us (5%)
  matrix products  4.52 us (2%)
    unnamed x3, waiting for transfers between devices  69.2 us
    all_gather x1, blocking collectives, body(): lax.all_gather(virtual_key, 'nodes', axis=0, tiled=True)  26.1 us
    all_gather x1, blocking collectives, body(): lax.all_gather(virtual_value, 'nodes', axis=0, tiled=True)  26 us
    unnamed x38, local copies, waits for them, and re-layouts  8.75 us
    ppermute x2, starting transfers between devices, extended(): after = lax.ppermute(leading, axis, down)  7.45 us
    all_to_all x1, starting transfers between devices, body(): lax.all_to_all(expand_sent, 'nodes', split_axis=0, concat_axis=0, tiled=T...  7.41 us
    all_gather x1, blocking collectives, body(): lax.all_gather(cotangent, 'mp', axis=1, tiled=True)  5.81 us
  transfers between devices with their start and end apart: 8, of which 1 were waited for; matrix products, arithmetic and copies ran while one was open for 8% of the time, Pallas kernels for 0%

commit v1 on v0

--- a/solution.py
+++ b/solution.py
@@ -4,6 +4,18 @@
 from jax.sharding import PartitionSpec as P
 
 HEADS = 8
+
+
+def prepare_sector_on_mesh(mine, ax_name="nodes"):
+    answer, f_now = (jax.lax.axis_size(ax_name), jax.lax.axis_index(ax_name))
+    arr_now, new = (mine, 1)
+    while new < answer:
+        fresh = jax.lax.ppermute(arr_now, ax_name, [(d, d ^ new) for d in range(answer)])
+        clean = jnp.concatenate([arr_now, fresh], axis=0)
+        b_now = jnp.concatenate([fresh, arr_now], axis=0)
+        arr_now = jnp.where(f_now & new == 0, clean, b_now)
+        new = 2 * new
+    return arr_now
 
 
 def extended(array, sides, width):
@@ -72,7 +84,7 @@
     )
     all_virtual_key, all_virtual_value = (
         lax.all_gather(virtual_key, "nodes", axis=0, tiled=True),
-        lax.all_gather(virtual_value, "nodes", axis=0, tiled=True),
+        prepare_sector_on_mesh(virtual_value),
     )
     virtual_count = all_virtual_key.shape[0]
     all_keys = jnp.concatenate(

time: 193 us -> 170 us (0.88)
  blocking collectives: 57.9 us -> 31.8 us
  waiting for transfers between devices: 69.2 us -> 71.9 us
    all_gather x1 -> x0, blocking collectives: 26 us -> none  [body(): lax.all_gather(virtual_value, 'nodes', axis=0, tiled=True)]
    ppermute x0 -> x3, starting transfers between devices: none -> 3.29 us  [prepare_sector_on_mesh(): jax.lax.ppermute(arr_now, ax_name, [(d, d ^ new) for d in range(answer)])]
    ppermute x0 -> x3, waiting for transfers between devices: none -> 2.69 us  [prepare_sector_on_mesh(): jax.lax.ppermute(arr_now, ax_name, [(d, d ^ new) for d in range(answer)])]
    all_to_all x1, starting transfers between devices: 7.41 us -> 5.01 us  [body(): lax.all_to_all(expand_sent, 'nodes', split_axis=0, concat_axis=0, tiled=T...]
  transfers between devices with their start and end apart: 8 -> 11, of which waited for: 1 -> 2; matrix products, arithmetic and copies ran while one was open for 8% -> 11% of each run, Pallas kernels for 0% -> 0%
where the time goes in v1:
time: 170 us; the launch traced here: 169 us
  waiting for transfers between devices  71.9 us (42%)
  blocking collectives  31.8 us (19%)
  starting transfers between devices  21.2 us (12%)
  between operations  16.5 us (10%)
  local copies, waits for them, and re-layouts  14.6 us (9%)
  other arithmetic  8.84 us (5%)
  matrix products  4.52 us (3%)
    unnamed x3, waiting for transfers between devices  69.2 us
    all_gather x1, blocking collectives, body(): lax.all_gather(virtual_key, 'nodes', axis=0, tiled=True)  26 us
    unnamed x38, local copies, waits for them, and re-layouts  8.71 us
    ppermute x2, starting transfers between devices, extended(): after = lax.ppermute(leading, axis, down)  7.45 us
    all_gather x1, blocking collectives, body(): lax.all_gather(cotangent, 'mp', axis=1, tiled=True)  5.81 us
    all_to_all x1, starting transfers between devices, body(): lax.all_to_all(expand_sent, 'nodes', split_axis=0, concat_axis=0, tiled=T...  5.01 us
  transfers between devices with their start and end apart: 11, of which 2 were waited for; matrix products, arithmetic and copies ran while one was open for 11% of the time, Pallas kernels for 0%

profile of v1, /device:TPU:0, one launch (start us, length us, event | category | flops | bytes accessed | tf_op | source)
XLA Modules:
  0.0 169.4 jit_solution(16647566277897796874)
XLA Ops:
  8.0 3.0 %collective-permute-start.2 = (bf16[8,128]{1,0:T(8,128)(2,1)}, bf16[8,128]{1,0:T(8,128)(2,1)S(1)}, u32[]{:S(2)}, u32[]{:S(2)}) collective-permute-start(bf16[8,128]{1,0:T(8,128)(2,1)} %param.18), channel_id=1, source_target_pairs={{0,4},{4,0},{8,12},{12,8},{16,20},{20,16},{24,28},{28,24},{1,5},{5... | collective-permute-start | bytes 6152 | tf_op jit(solution)/shard_map/ppermute | solution.py:13
  11.0 0.8 copy.38
  11.9 0.9 constant_dynamic-update-slice_fusion.1
  14.0 5.0 %all-to-all-start = ((bf16[8,2,256]{2,1,0:T(2,128)(2,1)}), bf16[8,2,256]{2,1,0:T(2,128)(2,1)S(1)}, u32[]{:S(2)}, u32[]{:S(2)}) async-start(bf16[8,2,256]{2,1,0:T(2,128)(2,1)} %reshape.142), calls=%async_computation | async-start | bytes 16384 | tf_op jit(solution)/shard_map/all_to_all | solution.py:82
  19.1 0.8 gather_fusion
  19.9 2.1 %collective-permute-start = (bf16[128,256]{1,0:T(8,128)(2,1)S(1)}, bf16[128,256]{1,0:T(8,128)(2,1)S(1)}, u32[]{:S(2)}, u32[]{:S(2)}) collective-permute-start(bf16[128,256]{1,0:T(8,128)(2,1)S(1)} %gather_fusion), channel_id=1, source_target_pairs={{0,4},{4,8},{8,12},{12,16},{16,20},{20,24},{24,28},{28,0},{1,5},{5... | collective-permute-start | bytes 196616 | tf_op jit(solution)/shard_map/ppermute | solution.py:28
  22.0 0.8 gather_fusion.1
  22.9 2.8 %collective-permute-start.1 = (bf16[128,256]{1,0:T(8,128)(2,1)S(1)}, bf16[128,256]{1,0:T(8,128)(2,1)S(1)}, u32[]{:S(2)}, u32[]{:S(2)}) collective-permute-start(bf16[128,256]{1,0:T(8,128)(2,1)S(1)} %gather_fusion.1), channel_id=1, source_target_pairs={{4,0},{8,4},{12,8},{16,12},{20,16},{24,20},{28,24},{0,28},{5,1},{9... | collective-permute-start | bytes 196616 | tf_op jit(solution)/shard_map/ppermute | solution.py:29
  29.2 5.8 %all_gather.7 = bf16[256,512]{1,0:T(8,128)(2,1)S(1)} all-gather(bf16[256,128]{1,0:T(8,128)(2,1)S(1)} %copy-done.3), channel_id=1, replica_groups=mesh['nodes'=8,'mp'=4] {'mp'}, dimensions={1}, use_global_device_ids=true | all-gather | bytes 327680 | tf_op jit(solution)/shard_map/all_gather | solution.py:103
  38.3 26.0 %all_gather.6 = bf16[64,128]{1,0:T(8,128)(2,1)S(1)} all-gather(bf16[8,128]{1,0:T(8,128)(2,1)S(1)} %copy-done.7), channel_id=1, replica_groups=mesh['nodes'=8,'mp'=4] {'nodes'}, dimensions={0}, use_global_device_ids=true | all-gather | bytes 18432 | tf_op jit(solution)/shard_map/all_gather | solution.py:86
  64.6 0.8 copy-done.1
  66.3 2.7 %collective-permute-done.4 = bf16[32,128]{1,0:T(8,128)(2,1)S(1)} collective-permute-done((bf16[32,128]{1,0:T(8,128)(2,1)S(1)}, bf16[32,128]{1,0:T(8,128)(2,1)S(1)}, u32[]{:S(2)}, u32[]{:S(2)}) %collective-permute-start.4) | collective-permute-done | bytes 8224 | tf_op jit(solution)/shard_map/ppermute | solution.py:13
  71.3 0.7 pad_maximum_fusion.6
  73.5 3.3 %all-to-all-start.1 = ((f32[8,2,256]{2,1,0:T(2,128)}), f32[8,2,256]{2,1,0:T(2,128)S(1)}, u32[]{:S(2)}, u32[]{:S(2)}) async-start(f32[8,2,256]{2,1,0:T(2,128)} %reshape.144), calls=%async_computation.2 | async-start | bytes 32768 | tf_op jit(solution)/shard_map/all_to_all | solution.py:158
  76.9 1.0 fusion.26
  79.1 0.8 copy.43
  80.0 4.7 %collective-permute-start.6 = (f32[128,256]{0,1:T(8,128)S(1)}, f32[128,256]{0,1:T(8,128)S(1)}, u32[]{:S(2)}, u32[]{:S(2)}) collective-permute-start(f32[128,256]{0,1:T(8,128)S(1)} %get-tuple-element.30), channel_id=1, source_target_pairs={{4,0},{8,4},{12,8},{16,12},{20,16},{24,20},{28,24},{0,28},{5,1},{9... | collective-permute-start | bytes 393224 | tf_op jit(solution)/shard_map/ppermute | solution.py:29
  84.7 68.7 %all-reduce.5.cloned.1.call-done = (f32[64,128]{0,1:T(8,128)}, f32[64,128]{0,1:T(8,128)}) async-done(((f32[64,128]{0,1:T(8,128)}, f32[64,128]{0,1:T(8,128)}), (f32[64,128]{0,1:T(8,128)}, f32[64,128]{0,1:T(8,128)})) %all-reduce.5.cloned.1.call-update) | async-done | bytes 65552
  153.4 0.9 constant_dynamic-slice_fusion.1
  156.0 1.4 scatter_fusion
  157.5 1.4 scatter_fusion.1
  158.9 0.8 scatter_fusion.2
  159.7 0.7 fusion.46
  160.5 1.5 convert_element_type.40
  (107 shorter events, 15.4 us)
Async XLA Ops:
  8.0 27.0 %copy-start = (bf16[128,512]{1,0:T(8,128)(2,1)S(1)}, bf16[128,512]{1,0:T(8,128)(2,1)}, u32[]{:S(2)}) copy-start(bf16[128,512]{1,0:T(8,128)(2,1)} %param.15) | copy-start | bytes 393220
  8.0 29.5 %collective-permute-start.2 = (bf16[8,128]{1,0:T(8,128)(2,1)}, bf16[8,128]{1,0:T(8,128)(2,1)S(1)}, u32[]{:S(2)}, u32[]{:S(2)}) collective-permute-start(bf16[8,128]{1,0:T(8,128)(2,1)} %param.18), channel_id=1, source_target_pairs={{0,4},{4,0},{8,12},{12,8},{16,20},{20,16},{24,28},{28,24},{1,5},{5... | collective-permute-start | bytes 6152 | tf_op jit(solution)/shard_map/ppermute | solution.py:13
  11.9 0.9 copy-start.2
  14.0 5.0 %copy-start.9 = (s32[1,2,128]{2,1,0:T(2,128)S(1)}, s32[1,2,128]{2,1,0:T(2,128)}, u32[]{:S(2)}) copy-start(s32[1,2,128]{2,1,0:T(2,128)} %param.19) | copy-start | bytes 3076
  14.0 50.4 %all-to-all-start = ((bf16[8,2,256]{2,1,0:T(2,128)(2,1)}), bf16[8,2,256]{2,1,0:T(2,128)(2,1)S(1)}, u32[]{:S(2)}, u32[]{:S(2)}) async-start(bf16[8,2,256]{2,1,0:T(2,128)(2,1)} %reshape.142), calls=%async_computation | async-start | bytes 16384 | tf_op jit(solution)/shard_map/all_to_all | solution.py:82
  19.9 44.5 %collective-permute-start = (bf16[128,256]{1,0:T(8,128)(2,1)S(1)}, bf16[128,256]{1,0:T(8,128)(2,1)S(1)}, u32[]{:S(2)}, u32[]{:S(2)}) collective-permute-start(bf16[128,256]{1,0:T(8,128)(2,1)S(1)} %gather_fusion), channel_id=1, source_target_pairs={{0,4},{4,8},{8,12},{12,16},{16,20},{20,24},{24,28},{28,0},{1,5},{5... | collective-permute-start | bytes 196616 | tf_op jit(solution)/shard_map/ppermute | solution.py:28
  22.0 3.6 %copy-start.5 = (s32[2,4]{1,0:T(2,128)S(1)}, s32[2,4]{1,0:T(2,128)}, u32[]{:S(2)}) copy-start(s32[2,4]{1,0:T(2,128)} %param.22) | copy-start | bytes 100
  22.0 7.2 %copy-start.3 = (bf16[256,128]{1,0:T(8,128)(2,1)S(1)}, bf16[256,128]{1,0:T(8,128)(2,1)}, u32[]{:S(2)}) copy-start(bf16[256,128]{1,0:T(8,128)(2,1)} %param.16) | copy-start | bytes 196612
  22.9 41.6 %collective-permute-start.1 = (bf16[128,256]{1,0:T(8,128)(2,1)S(1)}, bf16[128,256]{1,0:T(8,128)(2,1)S(1)}, u32[]{:S(2)}, u32[]{:S(2)}) collective-permute-start(bf16[128,256]{1,0:T(8,128)(2,1)S(1)} %gather_fusion.1), channel_id=1, source_target_pairs={{4,0},{8,4},{12,8},{16,12},{20,16},{24,20},{28,24},{0,28},{5,1},{9... | collective-permute-start | bytes 196616 | tf_op jit(solution)/shard_map/ppermute | solution.py:29
  25.7 0.7 copy-start.10
  26.5 0.7 copy-start.8
  35.6 0.7 copy-start.11
  37.5 0.7 copy-start.6
  37.6 0.8 copy-start.7
  38.1 26.2 %collective-permute-start.3 = (bf16[16,128]{1,0:T(8,128)(2,1)S(1)}, bf16[16,128]{1,0:T(8,128)(2,1)S(1)}, u32[]{:S(2)}, u32[]{:S(2)}) collective-permute-start(bf16[16,128]{1,0:T(8,128)(2,1)S(1)} %maximum_select_fusion.2), channel_id=1, source_target_pairs={{0,8},{4,12},{8,0},{12,4},{16,24},{20,28},{24,16},{28,20},{1,9},{5... | collective-permute-start | bytes 12296 | tf_op jit(solution)/shard_map/ppermute | solution.py:13
  64.3 4.6 %collective-permute-start.4 = (bf16[32,128]{1,0:T(8,128)(2,1)S(1)}, bf16[32,128]{1,0:T(8,128)(2,1)S(1)}, u32[]{:S(2)}, u32[]{:S(2)}) collective-permute-start(bf16[32,128]{1,0:T(8,128)(2,1)S(1)} %maximum_select_fusion.1), channel_id=1, source_target_pairs={{0,16},{4,20},{8,24},{12,28},{16,0},{20,4},{24,8},{28,12},{1,17},{... | collective-permute-start | bytes 24584 | tf_op jit(solution)/shard_map/ppermute | solution.py:13
  64.5 0.8 copy-start.1
  73.5 11.2 %all-to-all-start.1 = ((f32[8,2,256]{2,1,0:T(2,128)}), f32[8,2,256]{2,1,0:T(2,128)S(1)}, u32[]{:S(2)}, u32[]{:S(2)}) async-start(f32[8,2,256]{2,1,0:T(2,128)} %reshape.144), calls=%async_computation.2 | async-start | bytes 32768 | tf_op jit(solution)/shard_map/all_to_all | solution.py:158
  76.8 76.5 %all-reduce.5.cloned.1.call-start = ((), (), s32[]{:S(2)}) async-start(), calls=%async_computation.4 | async-start | bytes 262144
  77.9 82.5 %reduce-scatter.4.cloned.1.call-start = ((), (), s32[]{:S(2)}) async-start(), calls=%async_computation.3 | async-start | bytes 655360 | tf_op jit(solution)/shard_map/reduce_scatter | solution.py:148
  80.0 77.4 %collective-permute-start.6 = (f32[128,256]{0,1:T(8,128)S(1)}, f32[128,256]{0,1:T(8,128)S(1)}, u32[]{:S(2)}, u32[]{:S(2)}) collective-permute-start(f32[128,256]{0,1:T(8,128)S(1)} %get-tuple-element.30), channel_id=1, source_target_pairs={{4,0},{8,4},{12,8},{16,12},{20,16},{24,20},{28,24},{0,28},{5,1},{9... | collective-permute-start | bytes 393224 | tf_op jit(solution)/shard_map/ppermute | solution.py:29
  84.7 71.2 %collective-permute-start.5 = (f32[128,256]{0,1:T(8,128)S(1)}, f32[128,256]{0,1:T(8,128)S(1)}, u32[]{:S(2)}, u32[]{:S(2)}) collective-permute-start(f32[128,256]{0,1:T(8,128)S(1)} %get-tuple-element.31), channel_id=1, source_target_pairs={{0,4},{4,8},{8,12},{12,16},{16,20},{20,24},{24,28},{28,0},{1,5},{5... | collective-permute-start | bytes 393224 | tf_op jit(solution)/shard_map/ppermute | solution.py:28
  154.3 0.8 copy-start.4
Sparse Core Ops, SparseCore 0:
  82.1 71.2 all-reduce.4
Sparse Core Ops, SparseCore 1:
  80.9 22.9 reduce-scatter.3
